TPU v7x, 32 devices: a whole 2x2x4 slice. The times are simulated.
32 devices in a mesh: dp: 8 (over z, y), tensor: 4 (over x, core).
Axes of the slice: x: 2, y: 2, z: 4, core: 2. Of those that a mesh axis runs over, the one named last changes fastest.
Arguments:
- inputs: bfloat16 [16, 1024, 768], P('dp', 'tensor'), may hold values from -6 to 6
- segment_ids: int32 [16, 1024], P('dp'), may hold values from 0 to 11, never falling along the last dimension, each value on 1 to 512 neighbouring positions
- cotangent: bfloat16 [16, 1024, 768], P('dp', 'tensor'), may hold values from -6 to 6
- w_query: bfloat16 [768, 768], P(None, 'tensor'), may hold values from -0.21875 to 0.21875
- w_key: bfloat16 [768, 768], P(None, 'tensor'), may hold values from -0.21875 to 0.21875
- w_value: bfloat16 [768, 768], P(None, 'tensor'), may hold values from -0.21875 to 0.21875
- b_query: float32 [768], P('tensor'), may hold values from -3 to 3
- b_value: float32 [768], P('tensor'), may hold values from -3 to 3
- w_out: bfloat16 [768, 768], P('tensor'), may hold values from -1.25 to 1.25
- b_out: float32 [768], replicated, may hold values from -2 to 2
- gain_one: float32 [768], replicated, may hold values from 0.5 to 1.5
- shift_one: float32 [768], replicated, may hold values from -2 to 2
- w_up: bfloat16 [768, 3072], P(None, 'tensor'), may hold values from -0.21875 to 0.21875
- b_up: float32 [3072], P('tensor'), may hold values from -3 to 3
- w_down: bfloat16 [3072, 768], P('tensor'), may hold values from -0.109375 to 0.109375
- b_down: float32 [768], replicated, may hold values from -2 to 2
- gain_two: float32 [768], replicated, may hold values from 0.5 to 1.5
- shift_two: float32 [768], replicated, may hold values from -2 to 2
Outputs:
- output: bfloat16 [16, 1024, 768], P('dp', 'tensor')
- grad_input: float32 [16, 1024, 768], P('dp', 'tensor')
- grad_w_query: float32 [768, 768], P(None, 'tensor')
- grad_w_key: float32 [768, 768], P(None, 'tensor')
- grad_w_value: float32 [768, 768], P(None, 'tensor')
- grad_b_query: float32 [768], P('tensor')
- grad_b_value: float32 [768], P('tensor')
- grad_w_out: float32 [768, 768], P('tensor')
- grad_b_out: float32 [768], replicated
- grad_gain_one: float32 [768], replicated
- grad_shift_one: float32 [768], replicated
- grad_w_up: float32 [768, 3072], P(None, 'tensor')
- grad_b_up: float32 [3072], P('tensor')
- grad_w_down: float32 [3072, 768], P('tensor')
- grad_b_down: float32 [768], replicated
- grad_gain_two: float32 [768], replicated
- grad_shift_two: float32 [768], replicated
Inputs may be any that keep to these rules, and one draw needn't show every extreme that they name: `segment_ids`: along each sequence the ids never fall; each of the 12 documents of a sequence holds 1 to 512 consecutive tokens, and some document has exactly 512 of them.
All inputs are finite; a program needn't handle non-finite values.
Results may differ from a plain program's by a relative error of at most 0.018.
Values may be sent and summed in bfloat16 or wider, within the bound.
No kernel may reach another device: no remote copies, remote signals or barrier semaphores. Data moves between devices by JAX's collectives and lax.ppermute only.
A program may use at most 128 MiB of HBM per device.

v0:
```python
import math
import jax
import jax.numpy as jnp
from jax import lax
from jax.sharding import PartitionSpec as P

HEAD_DIM = 64
LAYER_EPSILON = 1e-05
BF = jnp.bfloat16
F32 = jnp.float32


def dot(left, right, contract):
    return lax.dot_general(left, right, (contract, ((), ())), preferred_element_type=F32)


def mm(left, right):
    return dot(left, right, ((1,), (0,)))


def mm_t(left, right):
    return dot(left, right, ((1,), (1,)))


def t_mm(left, right):
    return dot(left, right, ((0,), (0,)))


def normalize(rows):
    centred = rows - jnp.mean(rows, -1, keepdims=True)
    inverse = lax.rsqrt(jnp.mean(centred * centred, -1, keepdims=True) + LAYER_EPSILON)
    return (centred * inverse, inverse)


def norm_backward(grad, gain, normal, inverse):
    scaled = grad * gain
    mean = jnp.mean(scaled, -1, keepdims=True)
    mean_z = jnp.mean(scaled * normal, -1, keepdims=True)
    return (
        inverse * (scaled - mean - normal * mean_z),
        jnp.sum(grad * normal, 0),
        jnp.sum(grad, 0),
    )


def gelu_pair(u):
    root = math.sqrt(2 / math.pi)
    t = jnp.tanh(root * (u + 0.044715 * u * u * u))
    value = 0.5 * u * (1 + t)
    slope = 0.5 * (1 + t) + 0.5 * u * (1 - t * t) * root * (1 + 3 * 0.044715 * u * u)
    return (value, slope)


def attention_forward(query, keys, values, seg_q, seg_k):
    scores = jnp.einsum("qhd,khd->hqk", query, keys, preferred_element_type=F32) / math.sqrt(
        HEAD_DIM
    )
    masked = jnp.where((seg_q[:, None] == seg_k[None, :])[None], scores, -1e30)
    top = jnp.max(masked, -1, keepdims=True)
    exponent = jnp.exp(masked - top)
    total = jnp.sum(exponent, -1, keepdims=True)
    weights = (exponent / total).astype(BF)
    context = jnp.einsum("hqk,khd->qhd", weights, values, preferred_element_type=F32)
    return (context.astype(BF), top + jnp.log(total))


def attention_backward(query, keys, values, seg_q, seg_k, logsum, grad):
    scale = 1 / math.sqrt(HEAD_DIM)
    scores = jnp.einsum("qhd,khd->hqk", query, keys, preferred_element_type=F32) * scale
    masked = jnp.where((seg_q[:, None] == seg_k[None, :])[None], scores, -1e30)
    weights = jnp.exp(masked - logsum)
    grad_weights = jnp.einsum("qhd,khd->hqk", grad, values, preferred_element_type=F32)
    row = jnp.sum(weights * grad_weights, -1, keepdims=True)
    grad_scores = (weights * (grad_weights - row)).astype(BF)
    grad_query = jnp.einsum("hqk,khd->qhd", grad_scores, keys, preferred_element_type=F32) * scale
    grad_keys = jnp.einsum("hqk,qhd->khd", grad_scores, query, preferred_element_type=F32) * scale
    grad_values = jnp.einsum("hqk,qhd->khd", weights.astype(BF), grad, preferred_element_type=F32)
    return (grad_query.astype(BF), grad_keys, grad_values)


def shards(
    inputs,
    segment_ids,
    cotangent,
    w_query,
    w_key,
    w_value,
    b_query,
    b_value,
    w_out,
    b_out,
    gain_one,
    shift_one,
    w_up,
    b_up,
    w_down,
    b_down,
    gain_two,
    shift_two,
):
    ranks = lax.axis_size("tensor")
    rank = lax.axis_index("tensor")
    which = rank % 2
    rows = inputs.shape[1]
    half = 2 * rows
    width = w_query.shape[1]
    hidden_width = w_up.shape[1]
    model = inputs.shape[2]

    def inner(x):
        return lax.ppermute(x, "tensor", [(i, i ^ 1) for i in range(ranks)])

    def outer(x):
        return lax.ppermute(x, "tensor", [(i, i ^ 2) for i in range(ranks)])

    def to_sequence(x):
        kept = jnp.where(which == 0, x[0], x[1])
        got = inner(jnp.where(which == 0, x[1], x[0]))
        return jnp.where(which == 0, jnp.concatenate([kept, got]), jnp.concatenate([got, kept]))

    def from_sequence(x):
        low, high = (x[:rows], x[rows:])
        kept = jnp.where(which == 0, low, high)
        got = inner(jnp.where(which == 0, high, low))
        return jnp.where(which == 0, jnp.stack([kept, got]), jnp.stack([got, kept]))

    own_in = to_sequence(inputs)
    other_in = outer(own_in)
    own_cot = to_sequence(cotangent).astype(F32)

    def both(x, axis):
        return jnp.concatenate([x, inner(x)], axis)

    wqkv = both(jnp.concatenate([w_query, w_key, w_value], 1)[None], 0)
    wqkv = wqkv.reshape(2, model, 3, width).transpose(1, 2, 0, 3).reshape(model, 3 * 2 * width)
    bias = both(jnp.stack([b_query, b_value])[None], 0).transpose(1, 0, 2).reshape(2, 2 * width)
    bias_qkv = jnp.concatenate([bias[0], jnp.zeros((2 * width,), F32), bias[1]])
    w_out2 = both(w_out, 0)
    w_up2 = both(w_up, 1)
    b_up2 = both(b_up, 0)
    w_down2 = both(w_down, 0)
    segments = jnp.where(which == 0, segment_ids[0], segment_ids[1])
    first = jnp.where(rank // 2 == 0, segments[:half], segments[half:])
    second = jnp.where(rank // 2 == 0, segments[half:], segments[:half])
    seg = jnp.concatenate([first, second])
    heads = 2 * width // HEAD_DIM

    def project(x):
        return (mm(x, wqkv) + bias_qkv).astype(BF)

    qkv = [project(own_in), project(other_in)]

    def split(x):
        return [
            x[:, i * 2 * width : (i + 1) * 2 * width].reshape(-1, heads, HEAD_DIM) for i in range(3)
        ]

    pieces = [split(x) for x in qkv]
    keys = jnp.concatenate([pieces[0][1], pieces[1][1]])
    values = jnp.concatenate([pieces[0][2], pieces[1][2]])
    context_other, log_other = attention_forward(pieces[1][0], keys, values, second, seg)
    context_other = context_other.reshape(half, 2 * width)
    got = outer(mm(context_other, w_out2).astype(BF))
    context_own, log_own = attention_forward(pieces[0][0], keys, values, first, seg)
    context_own = context_own.reshape(half, 2 * width)
    attended = mm(context_own, w_out2) + got.astype(F32) + b_out
    normal_one, inverse_one = normalize(own_in.astype(F32) + attended)
    hidden_one = normal_one * gain_one + shift_one
    low_own = hidden_one.astype(BF)
    low_other = outer(low_own)

    def feed(low):
        value, slope = gelu_pair(mm(low, w_up2) + b_up2)
        return (value.astype(BF), slope)

    act_own, slope_own = feed(low_own)
    act_other, slope_other = feed(low_other)
    got = outer(mm(act_other, w_down2).astype(BF))
    branch = mm(act_own, w_down2) + got.astype(F32) + b_down
    normal_two, inverse_two = normalize(hidden_one + branch)
    output = (normal_two * gain_two + shift_two).astype(BF)
    grad_two, grad_gain_two, grad_shift_two = norm_backward(
        own_cot, gain_two, normal_two, inverse_two
    )
    gb_own = grad_two.astype(BF)
    grad_b_down = jnp.sum(gb_own.astype(F32), 0)
    gb_other = outer(gb_own)
    before_own = (mm_t(gb_own, w_down2) * slope_own).astype(BF)
    before_other = (mm_t(gb_other, w_down2) * slope_other).astype(BF)
    got = outer(mm_t(before_other, w_up2).astype(BF))
    grad_w_down = t_mm(act_own, gb_own) + t_mm(act_other, gb_other)
    grad_w_up = t_mm(low_own, before_own) + t_mm(low_other, before_other)
    grad_b_up = jnp.sum(before_own.astype(F32), 0) + jnp.sum(before_other.astype(F32), 0)
    grad_hidden = mm_t(before_own, w_up2) + got.astype(F32) + grad_two
    grad_one, grad_gain_one, grad_shift_one = norm_backward(
        grad_hidden, gain_one, normal_one, inverse_one
    )
    ga_own = grad_one.astype(BF)
    grad_b_out = jnp.sum(ga_own.astype(F32), 0)
    ga_other = outer(ga_own)

    def pair_sum(mine, theirs):
        return mine + inner(theirs.astype(BF)).astype(F32)

    grad_w_up = pair_sum(grad_w_up[:, :hidden_width], grad_w_up[:, hidden_width:])
    grad_w_down = pair_sum(grad_w_down[:hidden_width], grad_w_down[hidden_width:])
    feed_flat = jnp.concatenate([grad_w_up.astype(BF), grad_w_down.astype(BF)])
    feed_flat = lax.psum(feed_flat, "dp")
    gc_own = mm_t(ga_own, w_out2).astype(BF)
    gc_other = mm_t(ga_other, w_out2).astype(BF)
    grad_w_out = t_mm(context_own, ga_own) + t_mm(context_other, ga_other)
    shaped = (half, heads, HEAD_DIM)
    gq_own, gk_a, gv_a = attention_backward(
        pieces[0][0], keys, values, first, seg, log_own, gc_own.reshape(shaped)
    )
    gq_other, gk_b, gv_b = attention_backward(
        pieces[1][0], keys, values, second, seg, log_other, gc_other.reshape(shaped)
    )
    flat = (2 * half, 2 * width)
    gk = (gk_a + gk_b).astype(BF).reshape(flat)
    gv = (gv_a + gv_b).astype(BF).reshape(flat)
    gq_own = gq_own.reshape(half, 2 * width)
    gq_other = gq_other.reshape(half, 2 * width)
    gqkv_own = jnp.concatenate([gq_own, gk[:half], gv[:half]], 1)
    gqkv_other = jnp.concatenate([gq_other, gk[half:], gv[half:]], 1)
    got = outer(mm_t(gqkv_other, wqkv).astype(BF))
    grad_wqkv = t_mm(own_in, gqkv_own) + t_mm(other_in, gqkv_other)
    grad_bqkv = jnp.sum(gqkv_own.astype(F32), 0) + jnp.sum(gqkv_other.astype(F32), 0)
    grad_input = mm_t(gqkv_own, wqkv) + got.astype(F32) + grad_one
    by_part = grad_wqkv.reshape(model, 3, 2, width)
    grad_wqkv = pair_sum(
        by_part[:, :, 0].reshape(model, 3 * width), by_part[:, :, 1].reshape(model, 3 * width)
    )
    grad_w_out = pair_sum(grad_w_out[:width], grad_w_out[width:])
    attention_flat = jnp.concatenate(
        [grad_wqkv.astype(BF).reshape(-1, model), grad_w_out.astype(BF)]
    )
    attention_flat = lax.psum(attention_flat, "dp")
    bias_parts = grad_bqkv.reshape(3, 2, width)
    mine = jnp.concatenate([bias_parts[0, 0], bias_parts[2, 0], grad_b_up[:hidden_width]])
    theirs = jnp.concatenate([bias_parts[0, 1], bias_parts[2, 1], grad_b_up[hidden_width:]])
    small = lax.psum(mine + inner(theirs), "dp")
    shared = jnp.stack(
        [grad_b_out, grad_gain_one, grad_shift_one, grad_b_down, grad_gain_two, grad_shift_two]
    )
    shared = lax.psum(shared, ("dp", "tensor"))
    gw_qkv = attention_flat[: 3 * width].reshape(model, 3, width).astype(F32)
    return (
        from_sequence(output),
        from_sequence(grad_input),
        gw_qkv[:, 0],
        gw_qkv[:, 1],
        gw_qkv[:, 2],
        small[:width],
        small[width : 2 * width],
        attention_flat[3 * width :].astype(F32),
        shared[0],
        shared[1],
        shared[2],
        feed_flat[:model].astype(F32),
        small[2 * width :],
        feed_flat[model:].astype(F32),
        shared[3],
        shared[4],
        shared[5],
    )


def solution(mesh):
    tokens = P("dp", "tensor", None)
    columns = P(None, "tensor")
    lines = P("tensor", None)
    split = P("tensor")
    whole = P()
    return jax.shard_map(
        shards,
        mesh=mesh,
        in_specs=(tokens, P("dp", None), tokens, columns, columns, columns, split, split, lines)
        + (whole, whole, whole, columns, split, lines, whole, whole, whole),
        out_specs=(
            tokens,
            tokens,
            columns,
            columns,
            columns,
            split,
            split,
            lines,
            whole,
            whole,
            whole,
        )
        + (columns, split, lines, whole, whole, whole),
        check_vma=False,
    )
```

profile of v0, /device:TPU:0, one launch (start us, length us, event | category | flops | bytes accessed | tf_op | source)
XLA Modules:
  0.0 418.1 jit_solution(3931726033955160622)
XLA Ops:
  23.5 13.1 %collective-permute-done.3 = bf16[512,768]{1,0:T(8,128)(2,1)} collective-permute-done((bf16[512,768]{1,0:T(8,128)(2,1)S(1)}, bf16[512,768]{1,0:T(8,128)(2,1)}, u32[]{:S(2)}, u32[]{:S(2)}) %collective-permute-start.3) | collective-permute-done | bytes 786464 | tf_op jit(solution)/shard_map/ppermute | solution.py:114
  36.7 2.9 fusion.23
  42.2 3.6 fusion.62
  48.8 2.9 fusion.45
  59.3 3.5 fusion.46
  62.7 9.0 %collective-permute-done.5 = bf16[512,768]{1,0:T(8,128)(2,1)S(1)} collective-permute-done((bf16[512,768]{1,0:T(8,128)(2,1)S(1)}, bf16[512,768]{1,0:T(8,128)(2,1)S(1)}, u32[]{:S(2)}, u32[]{:S(2)}) %collective-permute-start.5) | collective-permute-done | bytes 786464 | tf_op jit(solution)/shard_map/ppermute | solution.py:114
  81.3 10.5 %collective-permute-done.9 = bf16[512,768]{1,0:T(8,128)(2,1)S(1)} collective-permute-done((bf16[512,768]{1,0:T(8,128)(2,1)S(1)}, bf16[512,768]{1,0:T(8,128)(2,1)S(1)}, u32[]{:S(2)}, u32[]{:S(2)}) %collective-permute-start.9) | collective-permute-done | bytes 786464 | tf_op jit(solution)/shard_map/ppermute | solution.py:114
  97.8 14.9 %collective-permute-done.10 = bf16[512,768]{1,0:T(8,128)(2,1)S(1)} collective-permute-done((bf16[512,768]{1,0:T(8,128)(2,1)S(1)}, bf16[512,768]{1,0:T(8,128)(2,1)S(1)}, u32[]{:S(2)}, u32[]{:S(2)}) %collective-permute-start.10) | collective-permute-done | bytes 786464 | tf_op jit(solution)/shard_map/ppermute | solution.py:114
  120.5 5.9 %convert_reduce_fusion.1 = (f32[1536]{0:T(1024)}, bf16[512,1536]{1,0:T(8,128)(2,1)}) fusion(f32[512,1536]{1,0:T(8,128)} %copy-done.74, bf16[512,768]{1,0:T(8,128)(2,1)S(1)} %get-tuple-element.52, bf16[1536,768]{1,0:T(8,128)(2,1)S(1)} %constant_dynamic-update-slice_fusion.7), kind=kOutput, calls=%fused_computation.46 | convolution fusion | flops 1224473088 | bytes 7870464 | tf_op jit(solution)/shard_map/dot_general | solution.py:14
  126.4 3.0 fusion.68
  129.4 3.9 fusion.51
  133.3 3.1 collective-permute-done.13
  136.4 5.3 %convert_reduce_fusion = (f32[1536]{0:T(1024)}, bf16[512,1536]{1,0:T(8,128)(2,1)S(1)}) fusion(f32[512,1536]{1,0:T(8,128)S(1)} %convolution_add_fusion.5, bf16[512,768]{1,0:T(8,128)(2,1)} %collective-permute-done.13, bf16[1536,768]{1,0:T(8,128)(2,1)} %copy-done.53), kind=kOutput, calls=%fused_computation.45 | convolution fusion | flops 1224473088 | bytes 7870464 | tf_op jit(solution)/shard_map/dot_general | solution.py:14
  141.7 4.6 %convolution_convert_fusion = bf16[512,768]{1,0:T(8,128)(2,1)} fusion(bf16[512,1536]{1,0:T(8,128)(2,1)S(1)} %get-tuple-element.109, bf16[768,1536]{1,0:T(8,128)(2,1)} %copy-done.54), kind=kOutput, calls=%fused_computation.95 | convolution fusion | flops 1208352768 | bytes 4718592 | tf_op jit(solution)/shard_map/dot_general | solution.py:14
  146.9 5.4 %convolution_add_fusion.1 = f32[1536,768]{1,0:T(8,128)S(1)} fusion(f32[1536,768]{1,0:T(8,128)} %fusion.51, bf16[512,768]{1,0:T(8,128)(2,1)} %collective-permute-done.13, f32[512,1536]{1,0:T(8,128)} %copy-done.5), kind=kOutput, calls=%fused_computation.27 | convolution fusion | flops 1216217088 | bytes 13369344 | tf_op jit(solution)/shard_map/dot_general | solution.py:14
  155.7 3.7 convolution_add_fusion.2
  162.5 4.8 %multiply_reduce_fusion.2 = (f32[768]{0:T(1024)}, f32[512]{0:T(512)S(1)}, f32[512]{0:T(512)S(1)}, f32[768]{0:T(1024)}, f32[512,768]{1,0:T(8,128)S(1)}) fusion(f32[512,768]{1,0:T(8,128)S(1)} %get-tuple-element.98, f32[512]{0:T(512)S(1)} %add_rsqrt_fusion.1, f32[512]{0:T(512)S(1)} %broadcast_multiply_fusion.5, f32[768]{0:T(1024)S(1)} %copy-done.60, ...), kind=kOutput, calls=%fused_computation.78 | convolution fusion | flops 1219360256 | bytes 10252289 | tf_op jit(solution)/shard_map/dot_general | solution.py:14
  173.6 7.5 %multiply_reduce_fusion.1 = (f32[6,512]{1,0:T(8,128)}, f32[6,512,1024]{2,1,0:T(8,128)}) fusion(f32[6,512,1024]{2,1,0:T(8,128)S(1)} %get-tuple-element.96, f32[6,512]{1,0:T(8,128)S(1)} %log_add_fusion.1, bf16[512,6,64]{0,2,1:T(8,128)(2,1)} %bitcast.173, bf16[512,6,64]{0,2,1:T(8,128)(2,1)S(1)} %bitcast.149, bf16[512,6,64]{0,2,1:T(8,128)(2,1)S(1)} %bitcast.144), kind=kOutput, calls=%fused_computation.4 | convolution fusion | flops 413660160 | bytes 26370048 | tf_op jit(solution)/shard_map/qhd,khd->hqk/dot_general | solution.py:72
  181.1 9.2 %multiply_convert_fusion.1 = bf16[6,512,1024]{2,1,0:T(8,128)(2,1)} fusion(f32[6,512,1024]{2,1,0:T(8,128)} %get-tuple-element.103, f32[6,512,1024]{2,1,0:T(8,128)S(1)} %get-tuple-element.96, f32[6,512]{1,0:T(8,128)} %get-tuple-element.102, f32[6,512]{1,0:T(8,128)S(1)} %log_add_fusion.1), kind=kLoop, calls=%fused_computation.3 | loop fusion | flops 12582912 | bytes 31481856 | tf_op jit(solution)/shard_map/convert_element_type | solution.py:74
  190.4 5.7 %fusion.43 = bf16[6,64,512]{2,1,0:T(8,128)(2,1)} fusion(bf16[6,512,1024]{2,1,0:T(8,128)(2,1)} %multiply_convert_fusion.1, bf16[512,6,64]{0,2,1:T(8,128)(2,1)S(1)} %bitcast.140, bf16[512,6,64]{0,2,1:T(8,128)(2,1)S(1)} %bitcast.136), kind=kOutput, calls=%fused_computation.105 | convolution fusion | flops 404619264 | bytes 7471104 | tf_op jit(solution)/shard_map/hqk,khd->qhd/dot_general | solution.py:75
  206.2 3.2 fusion.4
  209.4 7.2 %multiply_reduce_fusion = (f32[6,512]{1,0:T(8,128)S(1)}, f32[6,512,1024]{2,1,0:T(8,128)}) fusion(f32[6,512,1024]{2,1,0:T(8,128)S(1)} %get-tuple-element.94, f32[6,512]{1,0:T(8,128)S(1)} %log_add_fusion, bf16[512,6,64]{0,2,1:T(8,128)(2,1)} %bitcast.176, bf16[512,6,64]{0,2,1:T(8,128)(2,1)} %bitcast.147, bf16[512,6,64]{0,2,1:T(8,128)(2,1)S(1)} %bitcast.145), kind=kOutput, calls=%fused_computation.1 | convolution fusion | flops 413660160 | bytes 26370048 | tf_op jit(solution)/shard_map/qhd,khd->hqk/dot_general | solution.py:72
  216.6 3.6 fusion.39
  220.4 6.9 %multiply_convert_fusion = bf16[6,512,1024]{2,1,0:T(8,128)(2,1)S(1)} fusion(f32[6,512,1024]{2,1,0:T(8,128)} %get-tuple-element.105, f32[6,512,1024]{2,1,0:T(8,128)S(1)} %get-tuple-element.94, f32[6,512]{1,0:T(8,128)S(1)} %get-tuple-element.104, f32[6,512]{1,0:T(8,128)S(1)} %log_add_fusion), kind=kLoop, calls=%fused_computation | loop fusion | flops 12582912 | bytes 31481856 | tf_op jit(solution)/shard_map/convert_element_type | solution.py:74
  234.5 3.0 copy.63
  256.5 16.2 %collective-permute-done.16 = bf16[512,768]{1,0:T(8,128)(2,1)S(1)} collective-permute-done((bf16[512,768]{1,0:T(8,128)(2,1)S(1)}, bf16[512,768]{1,0:T(8,128)(2,1)S(1)}, u32[]{:S(2)}, u32[]{:S(2)}) %collective-permute-start.16) | collective-permute-done | bytes 786464 | tf_op jit(solution)/shard_map/ppermute | solution.py:114
  275.1 42.1 %psum.30 = f32[6,768]{1,0:T(8,128)S(1)} all-reduce(f32[6,768]{1,0:T(8,128)S(1)} %stack.75), channel_id=1, replica_groups=mesh['dp'=8,'tensor'=4] {'dp','tensor'}, use_global_device_ids=true, to_apply=%region_26.27 | all-reduce | flops 4608 | bytes 36864 | tf_op jit(solution)/shard_map/psum | solution.py:246
  319.1 21.8 %psum.29 = f32[1152]{0:T(1024)S(1)} all-reduce(f32[1152]{0:T(1024)S(1)} %add.245), channel_id=1, replica_groups=mesh['dp'=8,'tensor'=4] {'dp'}, use_global_device_ids=true, to_apply=%region_19.20 | all-reduce | flops 1152 | bytes 9216 | tf_op jit(solution)/shard_map/psum | solution.py:242
  344.8 45.4 %all-reduce.3.cloned.1.call-done = (bf16[768,768]{1,0:T(8,128)(2,1)}, bf16[1536,768]{1,0:T(8,128)(2,1)}) async-done(((bf16[768,768]{1,0:T(8,128)(2,1)}, bf16[1536,768]{1,0:T(8,128)(2,1)}), (bf16[768,768]{1,0:T(8,128)(2,1)}, bf16[1536,768]{1,0:T(8,128)(2,1)})) %all-reduce.3.cloned.1.call-update) | async-done | bytes 3538960 | tf_op jit(solution)/shard_map/psum | solution.py:238
  394.5 3.5 reshape.255
  398.0 2.9 fusion.54
  401.0 3.1 copy.67
  (312 shorter events, 121.0 us)
Async XLA Ops:
  7.2 383.0 %all-reduce.3.cloned.1.call-start = ((), (), s32[]{:S(2)}) async-start(), calls=%async_computation | async-start | bytes 7077888 | tf_op jit(solution)/shard_map/psum | solution.py:238
  8.0 6.6 %collective-permute-start.2 = (f32[1,2,192]{2,1,0:T(2,128)S(1)}, f32[1,2,192]{2,1,0:T(2,128)S(1)}, u32[]{:S(2)}, u32[]{:S(2)}) collective-permute-start(f32[1,2,192]{2,1,0:T(2,128)S(1)} %maximum_bitcast_fusion.1), channel_id=1, source_target_pairs={{0,1},{1,0},{2,3},{3,2},{4,5},{5,4},{6,7},{7,6},{8,9},{9,8},{10,11... | collective-permute-start | bytes 4616 | tf_op jit(solution)/shard_map/ppermute | solution.py:111
  8.6 69.0 %collective-permute-start.7 = (f32[768]{0:T(1024)}, f32[768]{0:T(1024)S(1)}, u32[]{:S(2)}, u32[]{:S(2)}) collective-permute-start(f32[768]{0:T(1024)} %param.31), channel_id=1, source_target_pairs={{0,1},{1,0},{2,3},{3,2},{4,5},{5,4},{6,7},{7,6},{8,9},{9,8},{10,11... | collective-permute-start | bytes 9224 | tf_op jit(solution)/shard_map/ppermute | solution.py:111
  8.6 7.1 %collective-permute-start.4 = (bf16[192,768]{1,0:T(8,128)(2,1)}, bf16[192,768]{1,0:T(8,128)(2,1)}, u32[]{:S(2)}, u32[]{:S(2)}) collective-permute-start(bf16[192,768]{1,0:T(8,128)(2,1)} %param.26), channel_id=1, source_target_pairs={{0,1},{1,0},{2,3},{3,2},{4,5},{5,4},{6,7},{7,6},{8,9},{9,8},{10,11... | collective-permute-start | bytes 884744 | tf_op jit(solution)/shard_map/ppermute | solution.py:111
  10.3 4.7 %collective-permute-start = (bf16[256,768]{1,0:T(8,128)(2,1)S(1)}, bf16[256,768]{1,0:T(8,128)(2,1)S(1)}, u32[]{:S(2)}, u32[]{:S(2)}) collective-permute-start(bf16[256,768]{1,0:T(8,128)(2,1)S(1)} %get-tuple-element.80), channel_id=1, source_target_pairs={{0,1},{1,0},{2,3},{3,2},{4,5},{5,4},{6,7},{7,6},{8,9},{9,8},{10,11... | collective-permute-start | bytes 1179656 | tf_op jit(solution)/shard_map/ppermute | solution.py:111
  11.5 7.9 %collective-permute-start.1 = (bf16[1,768,576]{1,2,0:T(8,128)(2,1)S(1)}, bf16[1,768,576]{1,2,0:T(8,128)(2,1)}, u32[]{:S(2)}, u32[]{:S(2)}) collective-permute-start(bf16[1,768,576]{1,2,0:T(8,128)(2,1)S(1)} %bitcast.161), channel_id=1, source_target_pairs={{0,1},{1,0},{2,3},{3,2},{4,5},{5,4},{6,7},{7,6},{8,9},{9,8},{10,11... | collective-permute-start | bytes 2654216 | tf_op jit(solution)/shard_map/ppermute | solution.py:111
  14.6 63.0 %collective-permute-start.6 = (bf16[768,768]{1,0:T(8,128)(2,1)}, bf16[768,768]{1,0:T(8,128)(2,1)}, u32[]{:S(2)}, u32[]{:S(2)}) collective-permute-start(bf16[768,768]{1,0:T(8,128)(2,1)} %param.30), channel_id=1, source_target_pairs={{0,1},{1,0},{2,3},{3,2},{4,5},{5,4},{6,7},{7,6},{8,9},{9,8},{10,11... | collective-permute-start | bytes 3538952 | tf_op jit(solution)/shard_map/ppermute | solution.py:111
  15.0 64.1 %collective-permute-start.8 = (bf16[768,768]{1,0:T(8,128)(2,1)}, bf16[768,768]{1,0:T(8,128)(2,1)}, u32[]{:S(2)}, u32[]{:S(2)}) collective-permute-start(bf16[768,768]{1,0:T(8,128)(2,1)} %param.32), channel_id=1, source_target_pairs={{0,1},{1,0},{2,3},{3,2},{4,5},{5,4},{6,7},{7,6},{8,9},{9,8},{10,11... | collective-permute-start | bytes 3538952 | tf_op jit(solution)/shard_map/ppermute | solution.py:111
  15.8 55.9 %copy-start.3 = (bf16[512,768]{1,0:T(8,128)(2,1)}, bf16[512,768]{1,0:T(8,128)(2,1)S(1)}, u32[]{:S(2)}) copy-start(bf16[512,768]{1,0:T(8,128)(2,1)S(1)} %maximum_select_fusion.1) | copy-start | bytes 2359300
  15.8 20.9 %collective-permute-start.3 = (bf16[512,768]{1,0:T(8,128)(2,1)S(1)}, bf16[512,768]{1,0:T(8,128)(2,1)}, u32[]{:S(2)}, u32[]{:S(2)}) collective-permute-start(bf16[512,768]{1,0:T(8,128)(2,1)S(1)} %maximum_select_fusion.1), channel_id=1, source_target_pairs={{0,2},{1,3},{2,0},{3,1},{4,6},{5,7},{6,4},{7,5},{8,10},{9,11},{10,... | collective-permute-start | bytes 2359304 | tf_op jit(solution)/shard_map/ppermute | solution.py:114
  23.3 167.0 %copy-start.14 = (bf16[512,384]{0,1:T(8,128)(2,1)}, bf16[512,384]{0,1:T(8,128)(2,1)S(1)}, u32[]{:S(2)}) copy-start(bf16[512,384]{0,1:T(8,128)(2,1)S(1)} %copy.60) | copy-start | bytes 1179652
  23.5 25.2 %copy-start.18 = (bf16[512,384]{0,1:T(8,128)(2,1)}, bf16[512,384]{0,1:T(8,128)(2,1)S(1)}, u32[]{:S(2)}) copy-start(bf16[512,384]{0,1:T(8,128)(2,1)S(1)} %copy.57) | copy-start | bytes 1179652
  42.2 148.1 %copy-start.16 = (bf16[512,384]{0,1:T(8,128)(2,1)}, bf16[512,384]{0,1:T(8,128)(2,1)S(1)}, u32[]{:S(2)}) copy-start(bf16[512,384]{0,1:T(8,128)(2,1)S(1)} %copy.61) | copy-start | bytes 1179652
  52.3 19.4 %collective-permute-start.5 = (bf16[512,768]{1,0:T(8,128)(2,1)S(1)}, bf16[512,768]{1,0:T(8,128)(2,1)S(1)}, u32[]{:S(2)}, u32[]{:S(2)}) collective-permute-start(bf16[512,768]{1,0:T(8,128)(2,1)S(1)} %convolution_convert_fusion.3), channel_id=1, source_target_pairs={{0,2},{1,3},{2,0},{3,1},{4,6},{5,7},{6,4},{7,5},{8,10},{9,11},{10,... | collective-permute-start | bytes 2359304 | tf_op jit(solution)/shard_map/ppermute | solution.py:114
  73.2 18.5 %collective-permute-start.9 = (bf16[512,768]{1,0:T(8,128)(2,1)S(1)}, bf16[512,768]{1,0:T(8,128)(2,1)S(1)}, u32[]{:S(2)}, u32[]{:S(2)}) collective-permute-start(bf16[512,768]{1,0:T(8,128)(2,1)S(1)} %fusion.38), channel_id=1, source_target_pairs={{0,2},{1,3},{2,0},{3,1},{4,6},{5,7},{6,4},{7,5},{8,10},{9,11},{10,... | collective-permute-start | bytes 2359304 | tf_op jit(solution)/shard_map/ppermute | solution.py:114
  74.8 40.6 %collective-permute-start.12 = (bf16[256,768]{1,0:T(8,128)(2,1)S(1)}, bf16[256,768]{1,0:T(8,128)(2,1)S(1)}, u32[]{:S(2)}, u32[]{:S(2)}) collective-permute-start(bf16[256,768]{1,0:T(8,128)(2,1)S(1)} %get-tuple-element.75), channel_id=1, source_target_pairs={{0,1},{1,0},{2,3},{3,2},{4,5},{5,4},{6,7},{7,6},{8,9},{9,8},{10,11... | collective-permute-start | bytes 1179656 | tf_op jit(solution)/shard_map/ppermute | solution.py:111
  81.2 39.2 %copy-start.53 = (bf16[1536,768]{1,0:T(8,128)(2,1)}, bf16[1536,768]{1,0:T(8,128)(2,1)S(1)}, u32[]{:S(2)}) copy-start(bf16[1536,768]{1,0:T(8,128)(2,1)S(1)} %constant_dynamic-update-slice_fusion.7) | copy-start | bytes 7077892
  93.1 43.3 %copy-start.5 = (f32[512,1536]{1,0:T(8,128)}, f32[512,1536]{1,0:T(8,128)S(1)}, u32[]{:S(2)}) copy-start(f32[512,1536]{1,0:T(8,128)S(1)} %convolution_add_fusion.5) | copy-start | bytes 9437188
  95.1 17.7 %collective-permute-start.10 = (bf16[512,768]{1,0:T(8,128)(2,1)S(1)}, bf16[512,768]{1,0:T(8,128)(2,1)S(1)}, u32[]{:S(2)}, u32[]{:S(2)}) collective-permute-start(bf16[512,768]{1,0:T(8,128)(2,1)S(1)} %convolution_convert_fusion.1), channel_id=1, source_target_pairs={{0,2},{1,3},{2,0},{3,1},{4,6},{5,7},{6,4},{7,5},{8,10},{9,11},{10,... | collective-permute-start | bytes 2359304 | tf_op jit(solution)/shard_map/ppermute | solution.py:114
  119.6 16.8 %collective-permute-start.13 = (bf16[512,768]{1,0:T(8,128)(2,1)S(1)}, bf16[512,768]{1,0:T(8,128)(2,1)}, u32[]{:S(2)}, u32[]{:S(2)}) collective-permute-start(bf16[512,768]{1,0:T(8,128)(2,1)S(1)} %get-tuple-element.52), channel_id=1, source_target_pairs={{0,2},{1,3},{2,0},{3,1},{4,6},{5,7},{6,4},{7,5},{8,10},{9,11},{10,... | collective-permute-start | bytes 2359304 | tf_op jit(solution)/shard_map/ppermute | solution.py:114
  146.3 16.2 %collective-permute-start.14 = (bf16[512,768]{1,0:T(8,128)(2,1)}, bf16[512,768]{1,0:T(8,128)(2,1)}, u32[]{:S(2)}, u32[]{:S(2)}) collective-permute-start(bf16[512,768]{1,0:T(8,128)(2,1)} %convolution_convert_fusion), channel_id=1, source_target_pairs={{0,2},{1,3},{2,0},{3,1},{4,6},{5,7},{6,4},{7,5},{8,10},{9,11},{10,... | collective-permute-start | bytes 2359304 | tf_op jit(solution)/shard_map/ppermute | solution.py:114
  153.5 47.6 %collective-permute-start.22 = (bf16[768,768]{1,0:T(8,128)(2,1)}, bf16[768,768]{1,0:T(8,128)(2,1)}, u32[]{:S(2)}, u32[]{:S(2)}) collective-permute-start(bf16[768,768]{1,0:T(8,128)(2,1)} %slice.341), channel_id=1, source_target_pairs={{0,1},{1,0},{2,3},{3,2},{4,5},{5,4},{6,7},{7,6},{8,9},{9,8},{10,11... | collective-permute-start | bytes 3538952 | tf_op jit(solution)/shard_map/ppermute | solution.py:111
  162.3 77.1 %collective-permute-start.21 = (bf16[768,768]{1,0:T(8,128)(2,1)}, bf16[768,768]{1,0:T(8,128)(2,1)}, u32[]{:S(2)}, u32[]{:S(2)}) collective-permute-start(bf16[768,768]{1,0:T(8,128)(2,1)} %slice.342), channel_id=1, source_target_pairs={{0,1},{1,0},{2,3},{3,2},{4,5},{5,4},{6,7},{7,6},{8,9},{9,8},{10,11... | collective-permute-start | bytes 3538952 | tf_op jit(solution)/shard_map/ppermute | solution.py:111
  172.4 31.4 %collective-permute-start.15 = (bf16[512,768]{1,0:T(8,128)(2,1)}, bf16[512,768]{1,0:T(8,128)(2,1)}, u32[]{:S(2)}, u32[]{:S(2)}) collective-permute-start(bf16[512,768]{1,0:T(8,128)(2,1)} %get-tuple-element.54), channel_id=1, source_target_pairs={{0,2},{1,3},{2,0},{3,1},{4,6},{5,7},{6,4},{7,5},{8,10},{9,11},{10,... | collective-permute-start | bytes 2359304 | tf_op jit(solution)/shard_map/ppermute | solution.py:114
  239.1 7.5 %collective-permute-start.18 = (bf16[768,576]{0,1:T(8,128)(2,1)S(1)}, bf16[768,576]{0,1:T(8,128)(2,1)S(1)}, u32[]{:S(2)}, u32[]{:S(2)}) collective-permute-start(bf16[768,576]{0,1:T(8,128)(2,1)S(1)} %bitcast.177), channel_id=1, source_target_pairs={{0,1},{1,0},{2,3},{3,2},{4,5},{5,4},{6,7},{7,6},{8,9},{9,8},{10,11... | collective-permute-start | bytes 2654216 | tf_op jit(solution)/shard_map/ppermute | solution.py:111
  243.6 3.0 collective-permute-start.19
  253.0 19.7 %collective-permute-start.16 = (bf16[512,768]{1,0:T(8,128)(2,1)S(1)}, bf16[512,768]{1,0:T(8,128)(2,1)S(1)}, u32[]{:S(2)}, u32[]{:S(2)}) collective-permute-start(bf16[512,768]{1,0:T(8,128)(2,1)S(1)} %convolution_convert_fusion.2), channel_id=1, source_target_pairs={{0,2},{1,3},{2,0},{3,1},{4,6},{5,7},{6,4},{7,5},{8,10},{9,11},{10,... | collective-permute-start | bytes 2359304 | tf_op jit(solution)/shard_map/ppermute | solution.py:114
  253.7 1.8 collective-permute-start.11
  274.0 43.2 %copy-start.45 = (bf16[512,6,64]{0,2,1:T(8,128)(2,1)S(1)}, bf16[512,6,64]{0,2,1:T(8,128)(2,1)}, u32[]{:S(2)}) copy-start(bf16[512,6,64]{0,2,1:T(8,128)(2,1)} %copy-done.43) | copy-start | bytes 1179652
  274.0 43.2 %copy-start.48 = (bf16[512,6,64]{0,2,1:T(8,128)(2,1)S(1)}, bf16[512,6,64]{0,2,1:T(8,128)(2,1)}, u32[]{:S(2)}) copy-start(bf16[512,6,64]{0,2,1:T(8,128)(2,1)} %copy-done.46) | copy-start | bytes 1179652
  275.0 67.1 %collective-permute-start.17 = (f32[256,768]{1,0:T(8,128)}, f32[256,768]{1,0:T(8,128)}, u32[]{:S(2)}, u32[]{:S(2)}) collective-permute-start(f32[256,768]{1,0:T(8,128)} %get-tuple-element.63), channel_id=1, source_target_pairs={{0,1},{1,0},{2,3},{3,2},{4,5},{5,4},{6,7},{7,6},{8,9},{9,8},{10,11... | collective-permute-start | bytes 2359304 | tf_op jit(solution)/shard_map/ppermute | solution.py:111
  317.9 1.2 collective-permute-start.20
  (70 other events, 390.9 us)
Sparse Core Ops, SparseCore 0:
  250.1 140.0 all-reduce.2
where the time goes:
time: 425 us; the launch traced here: 418 us
  waiting for transfers between devices  114 us (27%)
  matrix products  109 us (26%)
  blocking collectives  63.9 us (15%)
  other arithmetic  54.8 us (13%)
  local copies, waits for them, and re-layouts  46.4 us (11%)
  between operations  15.6 us (4%)
  starting transfers between devices  13.8 us (3%)
    ppermute x8, waiting for transfers between devices, outer(): return lax.ppermute(x, 'tensor', [(i, i ^ 2) for i in range(ranks)])  67.1 us
    dot_general x24, matrix products, dot(): lax.dot_general(left, right, (contract, ((), ())), preferred_element_type...  63.9 us
    psum x1, waiting for transfers between devices, shards(): attention_flat = lax.psum(attention_flat, 'dp')  45.4 us
    psum x1, blocking collectives, shards(): shared = lax.psum(shared, ('dp', 'tensor'))  42.1 us
    psum x1, blocking collectives, shards(): small = lax.psum(mine + inner(theirs), 'dp')  21.8 us
    convert_element_type x2, other arithmetic, attention_backward(): grad_scores = (weights * (grad_weights - row)).astype(BF)  16.1 us
    dot_general x2, matrix products, attention_backward(): jnp.einsum('qhd,khd->hqk', grad, values, preferred_element_type=F32)  14.7 us
    unnamed x161, local copies, waits for them, and re-layouts  10.7 us
  transfers between devices with their start and end apart: 24, of which 10 were waited for; matrix products, arithmetic and copies ran while one was open for 40% of the time, Pallas kernels for 0%

commit v1 on v0

--- a/solution.py
+++ b/solution.py
@@ -235,7 +235,11 @@
     attention_flat = jnp.concatenate(
         [grad_wqkv.astype(BF).reshape(-1, model), grad_w_out.astype(BF)]
     )
-    attention_flat = lax.psum(attention_flat, "dp")
+    attention_flat = attention_flat
+    for hop in (1, 2, 4):
+        attention_flat = attention_flat + lax.ppermute(
+            attention_flat, "dp", [(dev, dev ^ hop) for dev in range(8)]
+        )
     bias_parts = grad_bqkv.reshape(3, 2, width)
     mine = jnp.concatenate([bias_parts[0, 0], bias_parts[2, 0], grad_b_up[:hidden_width]])
     theirs = jnp.concatenate([bias_parts[0, 1], bias_parts[2, 1], grad_b_up[hidden_width:]])

time: 425 us -> 469 us (1.10)
  the two profiles are of different devices: /device:TPU:0 before, /device:TPU:10 now
where the time goes in v1:
time: 469 us; the launch traced here: 462 us
  blocking collectives  137 us (29%)
  matrix products  108 us (23%)
  waiting for transfers between devices  83.4 us (18%)
  other arithmetic  59.4 us (13%)
  local copies, waits for them, and re-layouts  46.8 us (10%)
  between operations  15.6 us (3%)
  starting transfers between devices  11 us (2%)
    psum x1, blocking collectives, shards(): small = lax.psum(mine + inner(theirs), 'dp')  82.1 us
    dot_general x24, matrix products, dot(): lax.dot_general(left, right, (contract, ((), ())), preferred_element_type...  64 us
    ppermute x8, waiting for transfers between devices, outer(): return lax.ppermute(x, 'tensor', [(i, i ^ 2) for i in range(ranks)])  55.8 us
    psum x1, blocking collectives, shards(): shared = lax.psum(shared, ('dp', 'tensor'))  55.3 us
    ppermute x3, waiting for transfers between devices, shards(): lax.ppermute(attention_flat, 'dp', [(dev, dev ^ hop) for dev in range(8)])  27.5 us
    convert_element_type x2, other arithmetic, attention_backward(): grad_scores = (weights * (grad_weights - row)).astype(BF)  16.1 us
    dot_general x2, matrix products, attention_backward(): jnp.einsum('qhd,khd->hqk', grad, values, preferred_element_type=F32)  14.9 us
    unnamed x153, local copies, waits for them, and re-layouts  9.9 us
  transfers between devices with their start and end apart: 27, of which 7 were waited for; matrix products, arithmetic and copies ran while one was open for 38% of the time, Pallas kernels for 0%

profile of v1, /device:TPU:10, one launch (start us, length us, event | category | flops | bytes accessed | tf_op | source)
XLA Modules:
  0.0 462.0 jit_solution(11783263948685904958)
XLA Ops:
  21.1 14.3 %collective-permute-done.3 = bf16[512,768]{1,0:T(8,128)(2,1)} collective-permute-done((bf16[512,768]{1,0:T(8,128)(2,1)S(1)}, bf16[512,768]{1,0:T(8,128)(2,1)}, u32[]{:S(2)}, u32[]{:S(2)}) %collective-permute-start.3) | collective-permute-done | bytes 786464 | tf_op jit(solution)/shard_map/ppermute | solution.py:114
  35.4 2.9 fusion.23
  41.0 3.6 fusion.63
  47.6 2.9 fusion.45
  56.8 3.5 fusion.46
  60.3 9.9 %collective-permute-done.5 = bf16[512,768]{1,0:T(8,128)(2,1)S(1)} collective-permute-done((bf16[512,768]{1,0:T(8,128)(2,1)S(1)}, bf16[512,768]{1,0:T(8,128)(2,1)S(1)}, u32[]{:S(2)}, u32[]{:S(2)}) %collective-permute-start.5) | collective-permute-done | bytes 786464 | tf_op jit(solution)/shard_map/ppermute | solution.py:114
  78.8 11.1 %collective-permute-done.9 = bf16[512,768]{1,0:T(8,128)(2,1)S(1)} collective-permute-done((bf16[512,768]{1,0:T(8,128)(2,1)S(1)}, bf16[512,768]{1,0:T(8,128)(2,1)S(1)}, u32[]{:S(2)}, u32[]{:S(2)}) %collective-permute-start.9) | collective-permute-done | bytes 786464 | tf_op jit(solution)/shard_map/ppermute | solution.py:114
  95.4 15.3 %collective-permute-done.10 = bf16[512,768]{1,0:T(8,128)(2,1)S(1)} collective-permute-done((bf16[512,768]{1,0:T(8,128)(2,1)S(1)}, bf16[512,768]{1,0:T(8,128)(2,1)S(1)}, u32[]{:S(2)}, u32[]{:S(2)}) %collective-permute-start.10) | collective-permute-done | bytes 786464 | tf_op jit(solution)/shard_map/ppermute | solution.py:114
  118.0 5.1 %convert_reduce_fusion.1 = (f32[1536]{0:T(1024)}, bf16[512,1536]{1,0:T(8,128)(2,1)S(1)}) fusion(f32[512,1536]{1,0:T(8,128)} %copy-done.72, bf16[512,768]{1,0:T(8,128)(2,1)S(1)} %get-tuple-element.50, bf16[1536,768]{1,0:T(8,128)(2,1)S(1)} %constant_dynamic-update-slice_fusion.7), kind=kOutput, calls=%fused_computation.46 | convolution fusion | flops 1224473088 | bytes 7870464 | tf_op jit(solution)/shard_map/dot_general | solution.py:14
  125.0 3.9 fusion.52
  128.9 5.0 %collective-permute-done.13 = bf16[512,768]{1,0:T(8,128)(2,1)S(1)} collective-permute-done((bf16[512,768]{1,0:T(8,128)(2,1)S(1)}, bf16[512,768]{1,0:T(8,128)(2,1)S(1)}, u32[]{:S(2)}, u32[]{:S(2)}) %collective-permute-start.13) | collective-permute-done | bytes 786464 | tf_op jit(solution)/shard_map/ppermute | solution.py:114
  133.9 5.8 %convert_reduce_fusion = (f32[1536]{0:T(1024)}, bf16[512,1536]{1,0:T(8,128)(2,1)S(1)}) fusion(f32[512,1536]{1,0:T(8,128)} %copy-done.5, bf16[512,768]{1,0:T(8,128)(2,1)S(1)} %collective-permute-done.13, bf16[1536,768]{1,0:T(8,128)(2,1)} %copy-done.51), kind=kOutput, calls=%fused_computation.45 | convolution fusion | flops 1224473088 | bytes 7870464 | tf_op jit(solution)/shard_map/dot_general | solution.py:14
  139.8 4.5 convolution_convert_fusion
  144.8 5.4 %convolution_add_fusion.1 = f32[1536,768]{1,0:T(8,128)S(1)} fusion(f32[1536,768]{1,0:T(8,128)} %fusion.52, bf16[512,768]{1,0:T(8,128)(2,1)} %copy-done.50, f32[512,1536]{1,0:T(8,128)} %copy-done.5), kind=kOutput, calls=%fused_computation.27 | convolution fusion | flops 1216217088 | bytes 13369344 | tf_op jit(solution)/shard_map/dot_general | solution.py:14
  153.6 3.7 convolution_add_fusion.2
  160.2 4.8 %multiply_reduce_fusion.2 = (f32[768]{0:T(1024)}, f32[512]{0:T(512)S(1)}, f32[512]{0:T(512)S(1)}, f32[768]{0:T(1024)}, f32[512,768]{1,0:T(8,128)S(1)}) fusion(f32[512,768]{1,0:T(8,128)S(1)} %get-tuple-element.96, f32[512]{0:T(512)S(1)} %add_rsqrt_fusion.1, f32[512]{0:T(512)S(1)} %broadcast_multiply_fusion.5, f32[768]{0:T(1024)S(1)} %copy-done.58, ...), kind=kOutput, calls=%fused_computation.78 | convolution fusion | flops 1219360256 | bytes 10252289 | tf_op jit(solution)/shard_map/dot_general | solution.py:14
  171.3 7.7 %multiply_reduce_fusion.1 = (f32[6,512]{1,0:T(8,128)}, f32[6,512,1024]{2,1,0:T(8,128)}) fusion(f32[6,512,1024]{2,1,0:T(8,128)S(1)} %get-tuple-element.94, f32[6,512]{1,0:T(8,128)S(1)} %log_add_fusion.1, bf16[512,6,64]{0,2,1:T(8,128)(2,1)} %bitcast.171, bf16[512,6,64]{0,2,1:T(8,128)(2,1)S(1)} %bitcast.147, bf16[512,6,64]{0,2,1:T(8,128)(2,1)S(1)} %bitcast.142), kind=kOutput, calls=%fused_computation.4 | convolution fusion | flops 413660160 | bytes 26370048 | tf_op jit(solution)/shard_map/qhd,khd->hqk/dot_general | solution.py:72
  179.1 9.2 %multiply_convert_fusion.1 = bf16[6,512,1024]{2,1,0:T(8,128)(2,1)} fusion(f32[6,512,1024]{2,1,0:T(8,128)} %get-tuple-element.101, f32[6,512,1024]{2,1,0:T(8,128)S(1)} %get-tuple-element.94, f32[6,512]{1,0:T(8,128)} %get-tuple-element.100, f32[6,512]{1,0:T(8,128)S(1)} %log_add_fusion.1), kind=kLoop, calls=%fused_computation.3 | loop fusion | flops 12582912 | bytes 31481856 | tf_op jit(solution)/shard_map/convert_element_type | solution.py:74
  188.3 5.7 %fusion.43 = bf16[6,64,512]{2,1,0:T(8,128)(2,1)} fusion(bf16[6,512,1024]{2,1,0:T(8,128)(2,1)} %multiply_convert_fusion.1, bf16[512,6,64]{0,2,1:T(8,128)(2,1)S(1)} %bitcast.138, bf16[512,6,64]{0,2,1:T(8,128)(2,1)S(1)} %bitcast.134), kind=kOutput, calls=%fused_computation.105 | convolution fusion | flops 404619264 | bytes 7471104 | tf_op jit(solution)/shard_map/hqk,khd->qhd/dot_general | solution.py:75
  200.3 3.2 fusion.4
  203.5 7.2 %multiply_reduce_fusion = (f32[6,512]{1,0:T(8,128)S(1)}, f32[6,512,1024]{2,1,0:T(8,128)}) fusion(f32[6,512,1024]{2,1,0:T(8,128)S(1)} %get-tuple-element.92, f32[6,512]{1,0:T(8,128)S(1)} %log_add_fusion, bf16[512,6,64]{0,2,1:T(8,128)(2,1)} %bitcast.174, bf16[512,6,64]{0,2,1:T(8,128)(2,1)} %bitcast.145, bf16[512,6,64]{0,2,1:T(8,128)(2,1)S(1)} %bitcast.143), kind=kOutput, calls=%fused_computation.1 | convolution fusion | flops 413660160 | bytes 26370048 | tf_op jit(solution)/shard_map/qhd,khd->hqk/dot_general | solution.py:72
  210.7 3.6 fusion.39
  214.5 6.9 %multiply_convert_fusion = bf16[6,512,1024]{2,1,0:T(8,128)(2,1)S(1)} fusion(f32[6,512,1024]{2,1,0:T(8,128)} %get-tuple-element.103, f32[6,512,1024]{2,1,0:T(8,128)S(1)} %get-tuple-element.92, f32[6,512]{1,0:T(8,128)S(1)} %get-tuple-element.102, f32[6,512]{1,0:T(8,128)S(1)} %log_add_fusion), kind=kLoop, calls=%fused_computation | loop fusion | flops 12582912 | bytes 31481856 | tf_op jit(solution)/shard_map/convert_element_type | solution.py:74
  228.7 3.0 copy.63
  251.7 27.5 %collective-permute-done.20 = bf16[768,768]{1,0:T(8,128)(2,1)} collective-permute-done((bf16[768,768]{1,0:T(8,128)(2,1)}, bf16[768,768]{1,0:T(8,128)(2,1)}, u32[]{:S(2)}, u32[]{:S(2)}) %collective-permute-start.20) | collective-permute-done | bytes 1179680 | tf_op jit(solution)/shard_map/ppermute | solution.py:240
  286.5 55.3 %psum.22 = f32[6,768]{1,0:T(8,128)} all-reduce(f32[6,768]{1,0:T(8,128)S(1)} %stack.75), channel_id=1, replica_groups=mesh['dp'=8,'tensor'=4] {'dp','tensor'}, use_global_device_ids=true, to_apply=%region_25.26 | all-reduce | flops 4608 | bytes 36864 | tf_op jit(solution)/shard_map/psum | solution.py:250
  347.6 82.1 %psum.21 = f32[1152]{0:T(1024)S(1)} all-reduce(f32[1152]{0:T(1024)S(1)} %add.255), channel_id=1, replica_groups=mesh['dp'=8,'tensor'=4] {'dp'}, use_global_device_ids=true, to_apply=%region_18.19 | all-reduce | flops 1152 | bytes 9216 | tf_op jit(solution)/shard_map/psum | solution.py:246
  431.0 3.2 maximum_select_fusion
  434.2 4.2 slice_convert_fusion.3
  440.9 3.5 reshape.255
  444.4 3.0 fusion.55
  447.4 3.0 copy.67
  (312 shorter events, 116.2 us)
Async XLA Ops:
  7.2 427.0 %all-reduce.2.cloned.1.call-start = ((), (), s32[]{:S(2)}) async-start(), calls=%async_computation | async-start | bytes 4718592 | tf_op jit(solution)/shard_map/psum | solution.py:208
  8.0 6.2 %collective-permute-start.2 = (f32[1,2,192]{2,1,0:T(2,128)S(1)}, f32[1,2,192]{2,1,0:T(2,128)S(1)}, u32[]{:S(2)}, u32[]{:S(2)}) collective-permute-start(f32[1,2,192]{2,1,0:T(2,128)S(1)} %maximum_bitcast_fusion.1), channel_id=1, source_target_pairs={{0,1},{1,0},{2,3},{3,2},{4,5},{5,4},{6,7},{7,6},{8,9},{9,8},{10,11... | collective-permute-start | bytes 4616 | tf_op jit(solution)/shard_map/ppermute | solution.py:111
  8.1 67.1 %collective-permute-start.7 = (f32[768]{0:T(1024)}, f32[768]{0:T(1024)S(1)}, u32[]{:S(2)}, u32[]{:S(2)}) collective-permute-start(f32[768]{0:T(1024)} %param.31), channel_id=1, source_target_pairs={{0,1},{1,0},{2,3},{3,2},{4,5},{5,4},{6,7},{7,6},{8,9},{9,8},{10,11... | collective-permute-start | bytes 9224 | tf_op jit(solution)/shard_map/ppermute | solution.py:111
  8.6 6.8 %collective-permute-start.4 = (bf16[192,768]{1,0:T(8,128)(2,1)}, bf16[192,768]{1,0:T(8,128)(2,1)}, u32[]{:S(2)}, u32[]{:S(2)}) collective-permute-start(bf16[192,768]{1,0:T(8,128)(2,1)} %param.26), channel_id=1, source_target_pairs={{0,1},{1,0},{2,3},{3,2},{4,5},{5,4},{6,7},{7,6},{8,9},{9,8},{10,11... | collective-permute-start | bytes 884744 | tf_op jit(solution)/shard_map/ppermute | solution.py:111
  9.8 5.1 %collective-permute-start = (bf16[256,768]{1,0:T(8,128)(2,1)S(1)}, bf16[256,768]{1,0:T(8,128)(2,1)S(1)}, u32[]{:S(2)}, u32[]{:S(2)}) collective-permute-start(bf16[256,768]{1,0:T(8,128)(2,1)S(1)} %get-tuple-element.78), channel_id=1, source_target_pairs={{0,1},{1,0},{2,3},{3,2},{4,5},{5,4},{6,7},{7,6},{8,9},{9,8},{10,11... | collective-permute-start | bytes 1179656 | tf_op jit(solution)/shard_map/ppermute | solution.py:111
  11.4 5.6 %collective-permute-start.1 = (bf16[1,768,576]{1,2,0:T(8,128)(2,1)S(1)}, bf16[1,768,576]{1,2,0:T(8,128)(2,1)}, u32[]{:S(2)}, u32[]{:S(2)}) collective-permute-start(bf16[1,768,576]{1,2,0:T(8,128)(2,1)S(1)} %bitcast.159), channel_id=1, source_target_pairs={{0,1},{1,0},{2,3},{3,2},{4,5},{5,4},{6,7},{7,6},{8,9},{9,8},{10,11... | collective-permute-start | bytes 2654216 | tf_op jit(solution)/shard_map/ppermute | solution.py:111
  14.2 61.0 %collective-permute-start.6 = (bf16[768,768]{1,0:T(8,128)(2,1)}, bf16[768,768]{1,0:T(8,128)(2,1)}, u32[]{:S(2)}, u32[]{:S(2)}) collective-permute-start(bf16[768,768]{1,0:T(8,128)(2,1)} %param.30), channel_id=1, source_target_pairs={{0,1},{1,0},{2,3},{3,2},{4,5},{5,4},{6,7},{7,6},{8,9},{9,8},{10,11... | collective-permute-start | bytes 3538952 | tf_op jit(solution)/shard_map/ppermute | solution.py:111
  14.9 61.7 %collective-permute-start.8 = (bf16[768,768]{1,0:T(8,128)(2,1)}, bf16[768,768]{1,0:T(8,128)(2,1)}, u32[]{:S(2)}, u32[]{:S(2)}) collective-permute-start(bf16[768,768]{1,0:T(8,128)(2,1)} %param.32), channel_id=1, source_target_pairs={{0,1},{1,0},{2,3},{3,2},{4,5},{5,4},{6,7},{7,6},{8,9},{9,8},{10,11... | collective-permute-start | bytes 3538952 | tf_op jit(solution)/shard_map/ppermute | solution.py:111
  15.4 54.8 %copy-start.3 = (bf16[512,768]{1,0:T(8,128)(2,1)}, bf16[512,768]{1,0:T(8,128)(2,1)S(1)}, u32[]{:S(2)}) copy-start(bf16[512,768]{1,0:T(8,128)(2,1)S(1)} %maximum_select_fusion.1) | copy-start | bytes 2359300
  15.4 20.0 %collective-permute-start.3 = (bf16[512,768]{1,0:T(8,128)(2,1)S(1)}, bf16[512,768]{1,0:T(8,128)(2,1)}, u32[]{:S(2)}, u32[]{:S(2)}) collective-permute-start(bf16[512,768]{1,0:T(8,128)(2,1)S(1)} %maximum_select_fusion.1), channel_id=1, source_target_pairs={{0,2},{1,3},{2,0},{3,1},{4,6},{5,7},{6,4},{7,5},{8,10},{9,11},{10,... | collective-permute-start | bytes 2359304 | tf_op jit(solution)/shard_map/ppermute | solution.py:114
  20.9 167.4 %copy-start.13 = (bf16[512,384]{0,1:T(8,128)(2,1)}, bf16[512,384]{0,1:T(8,128)(2,1)S(1)}, u32[]{:S(2)}) copy-start(bf16[512,384]{0,1:T(8,128)(2,1)S(1)} %copy.60) | copy-start | bytes 1179652
  41.0 147.3 %copy-start.15 = (bf16[512,384]{0,1:T(8,128)(2,1)}, bf16[512,384]{0,1:T(8,128)(2,1)S(1)}, u32[]{:S(2)}) copy-start(bf16[512,384]{0,1:T(8,128)(2,1)S(1)} %copy.61) | copy-start | bytes 1179652
  51.1 19.1 %collective-permute-start.5 = (bf16[512,768]{1,0:T(8,128)(2,1)S(1)}, bf16[512,768]{1,0:T(8,128)(2,1)S(1)}, u32[]{:S(2)}, u32[]{:S(2)}) collective-permute-start(bf16[512,768]{1,0:T(8,128)(2,1)S(1)} %convolution_convert_fusion.3), channel_id=1, source_target_pairs={{0,2},{1,3},{2,0},{3,1},{4,6},{5,7},{6,4},{7,5},{8,10},{9,11},{10,... | collective-permute-start | bytes 2359304 | tf_op jit(solution)/shard_map/ppermute | solution.py:114
  71.7 18.2 %collective-permute-start.9 = (bf16[512,768]{1,0:T(8,128)(2,1)S(1)}, bf16[512,768]{1,0:T(8,128)(2,1)S(1)}, u32[]{:S(2)}, u32[]{:S(2)}) collective-permute-start(bf16[512,768]{1,0:T(8,128)(2,1)S(1)} %fusion.38), channel_id=1, source_target_pairs={{0,2},{1,3},{2,0},{3,1},{4,6},{5,7},{6,4},{7,5},{8,10},{9,11},{10,... | collective-permute-start | bytes 2359304 | tf_op jit(solution)/shard_map/ppermute | solution.py:114
  72.4 40.9 %collective-permute-start.12 = (bf16[256,768]{1,0:T(8,128)(2,1)S(1)}, bf16[256,768]{1,0:T(8,128)(2,1)S(1)}, u32[]{:S(2)}, u32[]{:S(2)}) collective-permute-start(bf16[256,768]{1,0:T(8,128)(2,1)S(1)} %get-tuple-element.73), channel_id=1, source_target_pairs={{0,1},{1,0},{2,3},{3,2},{4,5},{5,4},{6,7},{7,6},{8,9},{9,8},{10,11... | collective-permute-start | bytes 1179656 | tf_op jit(solution)/shard_map/ppermute | solution.py:111
  78.8 39.2 %copy-start.51 = (bf16[1536,768]{1,0:T(8,128)(2,1)}, bf16[1536,768]{1,0:T(8,128)(2,1)S(1)}, u32[]{:S(2)}) copy-start(bf16[1536,768]{1,0:T(8,128)(2,1)S(1)} %constant_dynamic-update-slice_fusion.7) | copy-start | bytes 7077892
  93.3 17.4 %collective-permute-start.10 = (bf16[512,768]{1,0:T(8,128)(2,1)S(1)}, bf16[512,768]{1,0:T(8,128)(2,1)S(1)}, u32[]{:S(2)}, u32[]{:S(2)}) collective-permute-start(bf16[512,768]{1,0:T(8,128)(2,1)S(1)} %convolution_convert_fusion.1), channel_id=1, source_target_pairs={{0,2},{1,3},{2,0},{3,1},{4,6},{5,7},{6,4},{7,5},{8,10},{9,11},{10,... | collective-permute-start | bytes 2359304 | tf_op jit(solution)/shard_map/ppermute | solution.py:114
  117.5 16.4 %collective-permute-start.13 = (bf16[512,768]{1,0:T(8,128)(2,1)S(1)}, bf16[512,768]{1,0:T(8,128)(2,1)S(1)}, u32[]{:S(2)}, u32[]{:S(2)}) collective-permute-start(bf16[512,768]{1,0:T(8,128)(2,1)S(1)} %get-tuple-element.50), channel_id=1, source_target_pairs={{0,2},{1,3},{2,0},{3,1},{4,6},{5,7},{6,4},{7,5},{8,10},{9,11},{10,... | collective-permute-start | bytes 2359304 | tf_op jit(solution)/shard_map/ppermute | solution.py:114
  144.3 15.9 %collective-permute-start.14 = (bf16[512,768]{1,0:T(8,128)(2,1)}, bf16[512,768]{1,0:T(8,128)(2,1)}, u32[]{:S(2)}, u32[]{:S(2)}) collective-permute-start(bf16[512,768]{1,0:T(8,128)(2,1)} %convolution_convert_fusion), channel_id=1, source_target_pairs={{0,2},{1,3},{2,0},{3,1},{4,6},{5,7},{6,4},{7,5},{8,10},{9,11},{10,... | collective-permute-start | bytes 2359304 | tf_op jit(solution)/shard_map/ppermute | solution.py:114
  151.4 84.4 %collective-permute-start.25 = (bf16[768,768]{1,0:T(8,128)(2,1)}, bf16[768,768]{1,0:T(8,128)(2,1)}, u32[]{:S(2)}, u32[]{:S(2)}) collective-permute-start(bf16[768,768]{1,0:T(8,128)(2,1)} %slice.341), channel_id=1, source_target_pairs={{0,1},{1,0},{2,3},{3,2},{4,5},{5,4},{6,7},{7,6},{8,9},{9,8},{10,11... | collective-permute-start | bytes 3538952 | tf_op jit(solution)/shard_map/ppermute | solution.py:111
  160.1 83.7 %collective-permute-start.24 = (bf16[768,768]{1,0:T(8,128)(2,1)}, bf16[768,768]{1,0:T(8,128)(2,1)}, u32[]{:S(2)}, u32[]{:S(2)}) collective-permute-start(bf16[768,768]{1,0:T(8,128)(2,1)} %slice.342), channel_id=1, source_target_pairs={{0,1},{1,0},{2,3},{3,2},{4,5},{5,4},{6,7},{7,6},{8,9},{9,8},{10,11... | collective-permute-start | bytes 3538952 | tf_op jit(solution)/shard_map/ppermute | solution.py:111
  169.9 27.9 %collective-permute-start.15 = (bf16[512,768]{1,0:T(8,128)(2,1)}, bf16[512,768]{1,0:T(8,128)(2,1)}, u32[]{:S(2)}, u32[]{:S(2)}) collective-permute-start(bf16[512,768]{1,0:T(8,128)(2,1)} %get-tuple-element.52), channel_id=1, source_target_pairs={{0,2},{1,3},{2,0},{3,1},{4,6},{5,7},{6,4},{7,5},{8,10},{9,11},{10,... | collective-permute-start | bytes 2359304 | tf_op jit(solution)/shard_map/ppermute | solution.py:114
  233.4 5.4 %collective-permute-start.18 = (bf16[768,576]{0,1:T(8,128)(2,1)S(1)}, bf16[768,576]{0,1:T(8,128)(2,1)S(1)}, u32[]{:S(2)}, u32[]{:S(2)}) collective-permute-start(bf16[768,576]{0,1:T(8,128)(2,1)S(1)} %bitcast.175), channel_id=1, source_target_pairs={{0,1},{1,0},{2,3},{3,2},{4,5},{5,4},{6,7},{7,6},{8,9},{9,8},{10,11... | collective-permute-start | bytes 2654216 | tf_op jit(solution)/shard_map/ppermute | solution.py:111
  235.5 3.2 collective-permute-start.19
  242.2 36.9 %collective-permute-start.20 = (bf16[768,768]{1,0:T(8,128)(2,1)}, bf16[768,768]{1,0:T(8,128)(2,1)}, u32[]{:S(2)}, u32[]{:S(2)}) collective-permute-start(bf16[768,768]{1,0:T(8,128)(2,1)} %pad_maximum_fusion.4), channel_id=1, source_target_pairs={{0,4},{4,0},{8,12},{12,8},{16,20},{20,16},{24,28},{28,24},{1,5},{5... | collective-permute-start | bytes 3538952 | tf_op jit(solution)/shard_map/ppermute | solution.py:240
  248.2 34.5 %collective-permute-start.16 = (bf16[512,768]{1,0:T(8,128)(2,1)}, bf16[512,768]{1,0:T(8,128)(2,1)}, u32[]{:S(2)}, u32[]{:S(2)}) collective-permute-start(bf16[512,768]{1,0:T(8,128)(2,1)} %convolution_convert_fusion.2), channel_id=1, source_target_pairs={{0,2},{1,3},{2,0},{3,1},{4,6},{5,7},{6,4},{7,5},{8,10},{9,11},{10,... | collective-permute-start | bytes 2359304 | tf_op jit(solution)/shard_map/ppermute | solution.py:114
  251.5 31.2 %copy-start.8 = (bf16[6,64,512]{2,1,0:T(8,128)(2,1)S(1)}, bf16[6,64,512]{2,1,0:T(8,128)(2,1)}, u32[]{:S(2)}) copy-start(bf16[6,64,512]{2,1,0:T(8,128)(2,1)} %fusion.43) | copy-start | bytes 1179652
  251.6 30.1 %collective-permute-start.11 = (bf16[256,768]{1,0:T(8,128)(2,1)S(1)}, bf16[256,768]{1,0:T(8,128)(2,1)S(1)}, u32[]{:S(2)}, u32[]{:S(2)}) collective-permute-start(bf16[256,768]{1,0:T(8,128)(2,1)S(1)} %get-tuple-element.76), channel_id=1, source_target_pairs={{0,1},{1,0},{2,3},{3,2},{4,5},{5,4},{6,7},{7,6},{8,9},{9,8},{10,11... | collective-permute-start | bytes 1179656 | tf_op jit(solution)/shard_map/ppermute | solution.py:111
  280.8 61.0 %collective-permute-start.21 = (bf16[768,768]{1,0:T(8,128)(2,1)S(1)}, bf16[768,768]{1,0:T(8,128)(2,1)}, u32[]{:S(2)}, u32[]{:S(2)}) collective-permute-start(bf16[768,768]{1,0:T(8,128)(2,1)S(1)} %fusion.51), channel_id=1, source_target_pairs={{0,8},{4,12},{8,0},{12,4},{16,24},{20,28},{24,16},{28,20},{1,9},{5... | collective-permute-start | bytes 3538952 | tf_op jit(solution)/shard_map/ppermute | solution.py:240
  286.4 144.6 %collective-permute-start.17 = (f32[256,768]{1,0:T(8,128)}, f32[256,768]{1,0:T(8,128)}, u32[]{:S(2)}, u32[]{:S(2)}) collective-permute-start(f32[256,768]{1,0:T(8,128)} %get-tuple-element.61), channel_id=1, source_target_pairs={{0,1},{1,0},{2,3},{3,2},{4,5},{5,4},{6,7},{7,6},{8,9},{9,8},{10,11... | collective-permute-start | bytes 2359304 | tf_op jit(solution)/shard_map/ppermute | solution.py:111
  343.5 94.9 %collective-permute-start.22 = (bf16[768,768]{1,0:T(8,128)(2,1)S(1)}, bf16[768,768]{1,0:T(8,128)(2,1)S(1)}, u32[]{:S(2)}, u32[]{:S(2)}) collective-permute-start(bf16[768,768]{1,0:T(8,128)(2,1)S(1)} %add.250), channel_id=1, source_target_pairs={{0,16},{4,20},{8,24},{12,28},{16,0},{20,4},{24,8},{28,12},{1,17},{... | collective-permute-start | bytes 3538952 | tf_op jit(solution)/shard_map/ppermute | solution.py:240
  345.9 1.7 collective-permute-start.23
  (69 other events, 594.9 us)
Sparse Core Ops, SparseCore 0:
  250.4 155.2 all-reduce.1
